TPU v7x, 32 devices: a whole 2x2x4 slice. The times are simulated.
32 devices in a mesh: fields: 2 (over x), prow: 8 (over z, y), pcol: 2 (over core).
Axes of the slice: x: 2, y: 2, z: 4, core: 2. Of those that a mesh axis runs over, the one named last changes fastest.
Arguments:
- inverse_tiles: bfloat16 [32, 16, 256, 256], P(('fields', 'prow'), 'pcol'), parts along dimension 0, may hold values from -6 to 6
- panel_blocks: bfloat16 [4, 8, 256, 512], P('fields', 'prow', None, 'pcol'), parts along dimension 0, may hold values from -0.125 to 0.125
- diag_inverse: float32 [4, 512], P('fields', 'pcol'), parts along dimension 0, may hold values from 0.5 to 2
- structure: int32 [4, 8], P('fields'), parts along dimension 0, may hold values from 0 to 15, as said below
- block_slot: int32 [32], P('fields'), parts along dimension 0, may hold values from 0 to 15, each once
Outputs:
- sigma_new: bfloat16 [4, 16, 256, 512], P('fields', 'prow', None, 'pcol'), parts along dimension 0
- variances: float32 [4, 512], P('fields', 'pcol'), parts along dimension 0
There are 2 independent parts, one for each index of `fields`. A program takes and returns all parts, laid end to end along the dimension named above; each array names one. Nothing has to cross between parts.
Inputs may be any that keep to these rules, and one draw needn't show every extreme that they name: `structure`: each row lists 8 distinct row blocks in increasing order, and the last is always 16 - 1. `block_slot`: each slot is used by exactly one row block.
All inputs are finite; a program needn't handle non-finite values.
Results may differ from a plain program's by a relative error of at most 0.0006.
Values may be sent and summed in bfloat16 or wider, within the bound.
No kernel may reach another device: no remote copies, remote signals or barrier semaphores. Data moves between devices by JAX's collectives and lax.ppermute only.
A program may use at most 128 MiB of HBM per device.

v0:
```python
import jax
import jax.numpy as jnp
from jax import lax
from jax.sharding import PartitionSpec as P


def swapped(shard, axis, stride):
    return lax.ppermute(shard, axis, [(i, i ^ 1 << stride) for i in range(lax.axis_size(axis))])


def make_accumulate(selected, row_hits, piece):
    contrib = jnp.einsum("iskxy,skyw->sixw", selected, piece, preferred_element_type=jnp.float32)
    own_panel = jnp.einsum("sik,skxw->sixw", row_hits, piece, preferred_element_type=jnp.float32)
    return (contrib, own_panel)


def per_device(inverse_tiles, panel_blocks, diag_inverse, structure, block_slot):
    rows_here = inverse_tiles.shape[0]
    tile_size = inverse_tiles.shape[2]
    supernodes = panel_blocks.shape[0]
    positions = structure.shape[1]
    prow_index = lax.axis_index("prow")
    pcol_index = lax.axis_index("pcol")
    slot_of = block_slot[structure]
    own_rows = prow_index * rows_here + jnp.arange(rows_here, dtype=jnp.int32)
    row_match = slot_of[:, None, :] == own_rows[None, :, None]
    row_hits = row_match.astype(jnp.bfloat16)
    row_used = jnp.any(row_match, axis=2)
    partner = swapped(inverse_tiles, "pcol", 0)
    first_half = jnp.where(pcol_index == 0, inverse_tiles, partner)
    second_half = jnp.where(pcol_index == 0, partner, inverse_tiles)
    whole_rows = jnp.concatenate([first_half, second_half], axis=1)
    selected = jnp.take(whole_rows, slot_of.reshape(-1), axis=1)
    selected = selected.reshape(rows_here, supernodes, positions, tile_size, tile_size)
    summed, own_panel = make_accumulate(
        selected, row_hits, lax.all_gather(panel_blocks, "prow", axis=1, tiled=True)
    )
    sigma_rows = jnp.where(row_used[:, :, None, None], -summed, jnp.zeros((), jnp.float32))
    partial_value = jnp.sum(own_panel * sigma_rows, axis=(1, 2))
    correction = lax.psum(partial_value, "prow")
    variances = diag_inverse - correction
    return (sigma_rows.astype(jnp.bfloat16), variances)


def solution(mesh):
    in_specs = (
        P(("fields", "prow"), "pcol", None, None),
        P("fields", "prow", None, "pcol"),
        P("fields", "pcol"),
        P("fields", None),
        P("fields"),
    )
    out_specs = (P("fields", "prow", None, "pcol"), P("fields", "pcol"))
    return jax.shard_map(
        per_device, mesh=mesh, in_specs=in_specs, out_specs=out_specs, check_vma=False
    )
```

profile of v0, /device:TPU:0, one launch (start us, length us, event | category | flops | bytes accessed | tf_op | source)
XLA Modules:
  0.0 95.9 jit_solution(17099047433927221169)
XLA Ops:
  7.2 0.0 copy-start
  7.2 0.0 all-gather.2.cloned.1.call-start
  7.2 0.7 all-gather.2.cloned.1.call-update
  7.9 0.6 collective-permute-start
  8.5 0.7 compare_select_fusion.1
  9.2 0.1 reshape.53
  9.2 0.0 copy-done
  9.2 0.7 gather_fusion
  9.9 0.1 reshape.52
  10.0 0.2 compare_reduce_fusion
  10.2 2.3 %collective-permute-done = bf16[2,8,256,256]{3,2,1,0:T(8,128)(2,1)S(1)} collective-permute-done((bf16[2,8,256,256]{3,2,1,0:T(8,128)(2,1)}, bf16[2,8,256,256]{3,2,1,0:T(8,128)(2,1)S(1)}, u32[]{:S(2)}, u32[]{:S(2)}) %collective-permute-start) | collective-permute-done | bytes 2097184 | tf_op jit(solution)/shard_map/ppermute | solution.py:8
  12.5 1.9 %broadcast_select_fusion.1 = (bf16[2,8,256,256]{3,2,1,0:T(8,128)(2,1)S(1)}, bf16[2,8,256,256]{3,2,1,0:T(8,128)(2,1)S(1)}) fusion(bf16[2,8,256,256]{3,2,1,0:T(8,128)(2,1)} %param.5, bf16[2,8,256,256]{3,2,1,0:T(8,128)(2,1)S(1)} %collective-permute-done, pred[]{:T(512)S(6)} %eq.20), kind=kLoop, calls=%fused_computation.11 | loop fusion | flops 2097152 | bytes 8388609 | tf_op jit(solution)/shard_map/jit(_where)/select_n | solution.py:30
  14.3 2.3 %pad_maximum_fusion = bf16[2,16,256,256]{3,2,1,0:T(8,128)(2,1)} fusion(bf16[2,8,256,256]{3,2,1,0:T(8,128)(2,1)S(1)} %get-tuple-element.3, bf16[2,8,256,256]{3,2,1,0:T(8,128)(2,1)S(1)} %get-tuple-element.2), kind=kLoop, calls=%fused_computation.2 | loop fusion | flops 2097152 | bytes 8388608 | tf_op jit(solution)/shard_map/concatenate | solution.py:32
  16.7 4.9 %gather_fusion.1 = bf16[16,2,256,256]{3,2,1,0:T(8,128)(2,1)} fusion(bf16[2,16,256,256]{3,2,1,0:T(8,128)(2,1)} %pad_maximum_fusion, s32[1024]{0:T(1024)S(1)} %pad_clamp_fusion), kind=kCustom, calls=%fused_computation.1 | custom fusion | bytes 8388672 | tf_op jit(solution)/shard_map/jit(_take)/gather | solution.py:33
  21.6 40.4 %all-gather.2.cloned.1.call-done = bf16[2,8,256,256]{3,2,1,0:T(8,128)(2,1)} async-done(((bf16[2,1,256,256]{3,2,1,0:T(8,128)(2,1)}), bf16[2,8,256,256]{3,2,1,0:T(8,128)(2,1)}) %all-gather.2.cloned.1.call-update) | async-done | bytes 2097168 | tf_op jit(solution)/shard_map/all_gather | solution.py:36
  62.0 0.0 copy-start.1
  62.0 3.2 %fusion.3 = f32[2,2,256,256]{3,1,2,0:T(2,128)S(1)} fusion(bf16[2,8,256,256]{3,2,1,0:T(8,128)(2,1)} %all-gather.2.cloned.1.call-done, s32[2,8]{1,0:T(2,128)S(1)} %reshape.52, s32[2]{0:T(128)S(1)} %iota_add_fusion), kind=kOutput, calls=%fused_computation.7 | convolution fusion | flops 4194336 | bytes 3145800 | tf_op jit(solution)/shard_map/sik,skxw->sixw/dot_general | solution.py:13
  65.2 0.0 copy-done.1
  65.2 0.0 copy-start.2
  65.2 4.3 %fusion.15 = (f32[2,256]{1,0:T(2,128)S(1)}, bf16[2,2,256,256]{3,2,1,0:T(8,128)(2,1)}) fusion(f32[2,2,256,256]{3,1,2,0:T(2,128)S(1)} %fusion.3, bf16[2,8,256,256]{3,2,1,0:T(8,128)(2,1)S(1)} %copy-done.1, bf16[2,2,8,256,256]{4,3,0,2,1:T(8,128)(2,1)} %bitcast.32, pred[2,8]{1,0:T(4,128)(4,1)S(1)} %compare_and_fusion, pred[2,2]{1,0:T(4,128)(4,1)S(1)} %compare_reduce_fusion), kind=kOutput, calls=%fused_computation.16 | convolution fusion | flops 1077149184 | bytes 7866388 | tf_op jit(solution)/shard_map/iskxy,skyw->sixw/dot_general | solution.py:12
  69.5 19.0 %psum.7 = f32[2,256]{1,0:T(2,128)S(1)} all-reduce(f32[2,256]{1,0:T(2,128)S(1)} %get-tuple-element.4), channel_id=1, replica_groups=mesh['fields'=2,'prow'=8,'pcol'=2] {'prow'}, use_global_device_ids=true, to_apply=%region_2.3 | all-reduce | flops 512 | bytes 4096 | tf_op jit(solution)/shard_map/psum | solution.py:40
  88.5 0.0 copy-done.2
  88.5 0.6 sub.3
  (5 shorter events, 0.0 us)
Async XLA Ops:
  7.2 2.1 %copy-start = (s32[16]{0:T(128)S(1)}, s32[16]{0:T(128)}, u32[]{:S(2)}) copy-start(s32[16]{0:T(128)} %param.9) | copy-start | bytes 196
  7.2 54.8 %all-gather.2.cloned.1.call-start = ((), (), s32[]{:S(2)}) async-start(), calls=%async_computation | async-start | bytes 2359296 | tf_op jit(solution)/shard_map/all_gather | solution.py:36
  7.9 4.6 %collective-permute-start = (bf16[2,8,256,256]{3,2,1,0:T(8,128)(2,1)}, bf16[2,8,256,256]{3,2,1,0:T(8,128)(2,1)S(1)}, u32[]{:S(2)}, u32[]{:S(2)}) collective-permute-start(bf16[2,8,256,256]{3,2,1,0:T(8,128)(2,1)} %param.5), channel_id=1, source_target_pairs={{0,1},{1,0},{2,3},{3,2},{4,5},{5,4},{6,7},{7,6},{8,9},{9,8},{10,11... | collective-permute-start | bytes 6291464 | tf_op jit(solution)/shard_map/ppermute | solution.py:8
  62.0 3.2 %copy-start.1 = (bf16[2,8,256,256]{3,2,1,0:T(8,128)(2,1)S(1)}, bf16[2,8,256,256]{3,2,1,0:T(8,128)(2,1)}, u32[]{:S(2)}) copy-start(bf16[2,8,256,256]{3,2,1,0:T(8,128)(2,1)} %all-gather.2.cloned.1.call-done) | copy-start | bytes 6291460
  65.2 23.3 %copy-start.2 = (f32[2,256]{1,0:T(2,128)S(1)}, f32[2,256]{1,0:T(2,128)}, u32[]{:S(2)}) copy-start(f32[2,256]{1,0:T(2,128)} %param.7) | copy-start | bytes 6148
Sparse Core Ops, SparseCore 0:
  10.2 51.7 all-gather.1
where the time goes:
time: 96.1 us; the launch traced here: 95.9 us
  waiting for transfers between devices  43.3 us (45%)
  blocking collectives  19 us (20%)
  between operations  14.1 us (15%)
  matrix products  7.51 us (8%)
  local copies, waits for them, and re-layouts  5.78 us (6%)
  other arithmetic  5.67 us (6%)
    all_gather x1, waiting for transfers between devices, per_device(): lax.all_gather(panel_blocks, 'prow', axis=1, tiled=True)  40.4 us
    psum x1, blocking collectives, per_device(): correction = lax.psum(partial_value, 'prow')  19 us
    gather x1, local copies, waits for them, and re-layouts, per_device(): selected = jnp.take(whole_rows, slot_of.reshape(-1), axis=1)  4.94 us
    dot_general x1, matrix products, make_accumulate(): jnp.einsum('iskxy,skyw->sixw', selected, piece, preferred_element_type=jn...  4.32 us
    dot_general x1, matrix products, make_accumulate(): jnp.einsum('sik,skxw->sixw', row_hits, piece, preferred_element_type=jnp....  3.19 us
    concatenate x1, other arithmetic, per_device(): whole_rows = jnp.concatenate([first_half, second_half], axis=1)  2.33 us
    ppermute x1, waiting for transfers between devices, swapped(): lax.ppermute(shard, axis, [(i, i ^ 1 << stride) for i in range(lax.axis_s...  2.26 us
  transfers between devices with their start and end apart: 2, of which 2 were waited for; matrix products, arithmetic and copies ran while one was open for 11% of the time, Pallas kernels for 0%

commit v1 on v0

--- a/solution.py
+++ b/solution.py
@@ -2,6 +2,18 @@
 import jax.numpy as jnp
 from jax import lax
 from jax.sharding import PartitionSpec as P
+
+
+def ring_gather(array, axis, dim):
+    ways, here, lap = (lax.axis_size(axis), lax.axis_index(axis), array.shape[dim])
+    dims = [n * ways if d == dim else n for d, n in enumerate(array.shape)]
+    full = lax.dynamic_update_slice_in_dim(
+        jnp.zeros(dims, array.dtype), array, here * lap, axis=dim
+    )
+    for far in range(1, ways):
+        array = lax.ppermute(array, axis, [(d, (d + 1) % ways) for d in range(ways)])
+        full = lax.dynamic_update_slice_in_dim(full, array, (here - far) % ways * lap, axis=dim)
+    return full
 
 
 def swapped(shard, axis, stride):
@@ -32,9 +44,7 @@
     whole_rows = jnp.concatenate([first_half, second_half], axis=1)
     selected = jnp.take(whole_rows, slot_of.reshape(-1), axis=1)
     selected = selected.reshape(rows_here, supernodes, positions, tile_size, tile_size)
-    summed, own_panel = make_accumulate(
-        selected, row_hits, lax.all_gather(panel_blocks, "prow", axis=1, tiled=True)
-    )
+    summed, own_panel = make_accumulate(selected, row_hits, ring_gather(panel_blocks, "prow", 1))
     sigma_rows = jnp.where(row_used[:, :, None, None], -summed, jnp.zeros((), jnp.float32))
     partial_value = jnp.sum(own_panel * sigma_rows, axis=(1, 2))
     correction = lax.psum(partial_value, "prow")

time: 96.1 us -> 162 us (1.69)
  local copies, waits for them, and re-layouts: 5.78 us -> 70 us
  between operations: 14.1 us -> 1.06 us
  waiting for transfers between devices: 43.3 us -> 54.9 us
  blocking collectives: 19 us -> 21.7 us
  starting transfers between devices: 0.6 us -> 3.07 us
  matrix products: 7.51 us -> 5.06 us
    dynamic_update_slice x0 -> x8, local copies, waits for them, and re-layouts: none -> 57.1 us  [the longest x7 49.9 us: ring_gather(): lax.dynamic_update_slice_in_dim(full, array, (here - far) % ways * lap, a...]
    ppermute x0 -> x7, waiting for transfers between devices: none -> 54.9 us  [ring_gather(): lax.ppermute(array, axis, [(d, (d + 1) % ways) for d in range(ways)])]
    all_gather x1 -> x0, waiting for transfers between devices: 40.4 us -> none  [per_device(): lax.all_gather(panel_blocks, 'prow', axis=1, tiled=True)]
    ppermute x0 -> x7, local copies, waits for them, and re-layouts: none -> 4.75 us  [ring_gather(): lax.ppermute(array, axis, [(d, (d + 1) % ways) for d in range(ways)])]
    ppermute x0 -> x7, starting transfers between devices: none -> 3.06 us  [ring_gather(): lax.ppermute(array, axis, [(d, (d + 1) % ways) for d in range(ways)])]
    psum x1, blocking collectives: 19 us -> 21.7 us  [per_device(): correction = lax.psum(partial_value, 'prow')]
    dot_general x1, matrix products: 3.19 us -> 0.76 us  [make_accumulate(): jnp.einsum('sik,skxw->sixw', row_hits, piece, preferred_element_type=jnp....]
    ppermute x1, waiting for transfers between devices: 2.26 us -> 0.01 us  [swapped(): lax.ppermute(shard, axis, [(i, i ^ 1 << stride) for i in range(lax.axis_s...]
  transfers between devices with their start and end apart: 2 -> 8, of which waited for: 2 -> 6; matrix products, arithmetic and copies ran while one was open for 11% -> 41% of each run, Pallas kernels for 0% -> 0%
where the time goes in v1:
time: 162 us; the launch traced here: 161 us
  local copies, waits for them, and re-layouts  70 us (43%)
  waiting for transfers between devices  54.9 us (34%)
  blocking collectives  21.7 us (13%)
  other arithmetic  5.64 us (3%)
  matrix products  5.06 us (3%)
  starting transfers between devices  3.07 us (2%)
    ppermute x7, waiting for transfers between devices, ring_gather(): lax.ppermute(array, axis, [(d, (d + 1) % ways) for d in range(ways)])  54.9 us
    dynamic_update_slice x7, local copies, waits for them, and re-layouts, ring_gather(): lax.dynamic_update_slice_in_dim(full, array, (here - far) % ways * lap, a...  49.9 us
    psum x1, blocking collectives, per_device(): correction = lax.psum(partial_value, 'prow')  21.7 us
    dynamic_update_slice x1, local copies, waits for them, and re-layouts, ring_gather(): lax.dynamic_update_slice_in_dim(jnp.zeros(dims, array.dtype), array, here...  7.13 us
    gather x1, local copies, waits for them, and re-layouts, per_device(): selected = jnp.take(whole_rows, slot_of.reshape(-1), axis=1)  4.98 us
    ppermute x7, local copies, waits for them, and re-layouts, ring_gather(): lax.ppermute(array, axis, [(d, (d + 1) % ways) for d in range(ways)])  4.75 us
    dot_general x1, matrix products, make_accumulate(): jnp.einsum('iskxy,skyw->sixw', selected, piece, preferred_element_type=jn...  4.31 us
  transfers between devices with their start and end apart: 8, of which 6 were waited for; matrix products, arithmetic and copies ran while one was open for 41% of the time, Pallas kernels for 0%

profile of v1, /device:TPU:0, one launch (start us, length us, event | category | flops | bytes accessed | tf_op | source)
XLA Modules:
  0.0 161.4 jit_solution(7169499935429212717)
XLA Ops:
  0.6 3.0 %collective-permute-start.1 = (bf16[2,1,256,256]{3,2,1,0:T(8,128)(2,1)}, bf16[2,1,256,256]{3,2,1,0:T(8,128)(2,1)S(1)}, u32[]{:S(2)}, u32[]{:S(2)}) collective-permute-start(bf16[2,1,256,256]{3,2,1,0:T(8,128)(2,1)} %param.6), channel_id=1, source_target_pairs={{0,2},{2,4},{4,6},{6,8},{8,10},{10,12},{12,14},{14,0},{1,3},{3,5},... | collective-permute-start | bytes 786440 | tf_op jit(solution)/shard_map/ppermute | solution.py:14
  3.7 9.6 %collective-permute-done.1 = bf16[2,1,256,256]{3,2,1,0:T(8,128)(2,1)S(1)} collective-permute-done((bf16[2,1,256,256]{3,2,1,0:T(8,128)(2,1)}, bf16[2,1,256,256]{3,2,1,0:T(8,128)(2,1)S(1)}, u32[]{:S(2)}, u32[]{:S(2)}) %collective-permute-start.1) | collective-permute-done | bytes 262176 | tf_op jit(solution)/shard_map/ppermute | solution.py:14
  13.3 10.2 %collective-permute-done.2 = bf16[2,1,256,256]{3,2,1,0:T(8,128)(2,1)S(1)} collective-permute-done((bf16[2,1,256,256]{3,2,1,0:T(8,128)(2,1)S(1)}, bf16[2,1,256,256]{3,2,1,0:T(8,128)(2,1)S(1)}, u32[]{:S(2)}, u32[]{:S(2)}) %collective-permute-start.2) | collective-permute-done | bytes 262176 | tf_op jit(solution)/shard_map/ppermute | solution.py:14
  23.4 9.3 %collective-permute-done.3 = bf16[2,1,256,256]{3,2,1,0:T(8,128)(2,1)S(1)} collective-permute-done((bf16[2,1,256,256]{3,2,1,0:T(8,128)(2,1)S(1)}, bf16[2,1,256,256]{3,2,1,0:T(8,128)(2,1)S(1)}, u32[]{:S(2)}, u32[]{:S(2)}) %collective-permute-start.3) | collective-permute-done | bytes 262176 | tf_op jit(solution)/shard_map/ppermute | solution.py:14
  32.7 9.1 %collective-permute-done.4 = bf16[2,1,256,256]{3,2,1,0:T(8,128)(2,1)S(1)} collective-permute-done((bf16[2,1,256,256]{3,2,1,0:T(8,128)(2,1)S(1)}, bf16[2,1,256,256]{3,2,1,0:T(8,128)(2,1)S(1)}, u32[]{:S(2)}, u32[]{:S(2)}) %collective-permute-start.4) | collective-permute-done | bytes 262176 | tf_op jit(solution)/shard_map/ppermute | solution.py:14
  41.8 0.7 compare_select_fusion.1
  42.6 0.7 gather_fusion
  43.3 7.5 %collective-permute-done.5 = bf16[2,1,256,256]{3,2,1,0:T(8,128)(2,1)S(1)} collective-permute-done((bf16[2,1,256,256]{3,2,1,0:T(8,128)(2,1)S(1)}, bf16[2,1,256,256]{3,2,1,0:T(8,128)(2,1)S(1)}, u32[]{:S(2)}, u32[]{:S(2)}) %collective-permute-start.5) | collective-permute-done | bytes 262176 | tf_op jit(solution)/shard_map/ppermute | solution.py:14
  51.1 9.3 %collective-permute-done.6 = bf16[2,1,256,256]{3,2,1,0:T(8,128)(2,1)} collective-permute-done((bf16[2,1,256,256]{3,2,1,0:T(8,128)(2,1)S(1)}, bf16[2,1,256,256]{3,2,1,0:T(8,128)(2,1)}, u32[]{:S(2)}, u32[]{:S(2)}) %collective-permute-start.6) | collective-permute-done | bytes 262176 | tf_op jit(solution)/shard_map/ppermute | solution.py:14
  60.5 1.4 copy.19
  62.1 7.1 %dynamic_update_slice.24 = bf16[2,8,256,256]{3,1,2,0:T(8,128)(2,1)S(1)} dynamic-update-slice(bf16[2,8,256,256]{3,1,2,0:T(8,128)(2,1)S(1)} %broadcast_in_dim.35, bf16[2,1,256,256]{3,1,2,0:T(2,128)(2,1)S(1)} %copy.19, s32[]{:T(128)} %constant.72.clone.1, s32[]{:T(128)S(6)} %select_n.103, s32[]{:T(128)} %constant.72.clone.1, s32[]{:T(128)} %constant.72.clone.1) | dynamic-update-slice | bytes 524292 | tf_op jit(solution)/shard_map/dynamic_update_slice | solution.py:10
  69.2 0.4 copy.20
  69.6 7.1 %dynamic_update_slice.25 = bf16[2,8,256,256]{3,1,2,0:T(8,128)(2,1)S(1)} dynamic-update-slice(bf16[2,8,256,256]{3,1,2,0:T(8,128)(2,1)S(1)} %dynamic_update_slice.24, bf16[2,1,256,256]{3,1,2,0:T(2,128)(2,1)S(1)} %copy.20, s32[]{:T(128)} %constant.72.clone.1, s32[]{:T(128)S(6)} %select_n.105, s32[]{:T(128)} %constant.72.clone.1, s32[]{:T(128)} %constant.72.clone.1) | dynamic-update-slice | bytes 524292 | tf_op jit(solution)/shard_map/dynamic_update_slice | solution.py:15
  76.8 0.4 copy.21
  77.2 7.1 %dynamic_update_slice.26 = bf16[2,8,256,256]{3,1,2,0:T(8,128)(2,1)S(1)} dynamic-update-slice(bf16[2,8,256,256]{3,1,2,0:T(8,128)(2,1)S(1)} %dynamic_update_slice.25, bf16[2,1,256,256]{3,1,2,0:T(2,128)(2,1)S(1)} %copy.21, s32[]{:T(128)} %constant.72.clone.1, s32[]{:T(128)S(6)} %select_n.107, s32[]{:T(128)} %constant.72.clone.1, s32[]{:T(128)} %constant.72.clone.1) | dynamic-update-slice | bytes 524292 | tf_op jit(solution)/shard_map/dynamic_update_slice | solution.py:15
  84.4 0.4 copy.22
  84.8 7.1 %dynamic_update_slice.27 = bf16[2,8,256,256]{3,1,2,0:T(8,128)(2,1)S(1)} dynamic-update-slice(bf16[2,8,256,256]{3,1,2,0:T(8,128)(2,1)S(1)} %dynamic_update_slice.26, bf16[2,1,256,256]{3,1,2,0:T(2,128)(2,1)S(1)} %copy.22, s32[]{:T(128)} %constant.72.clone.1, s32[]{:T(128)S(6)} %select_n.109, s32[]{:T(128)} %constant.72.clone.1, s32[]{:T(128)} %constant.72.clone.1) | dynamic-update-slice | bytes 524292 | tf_op jit(solution)/shard_map/dynamic_update_slice | solution.py:15
  91.9 0.4 copy.23
  92.3 7.1 %dynamic_update_slice.28 = bf16[2,8,256,256]{3,1,2,0:T(8,128)(2,1)S(1)} dynamic-update-slice(bf16[2,8,256,256]{3,1,2,0:T(8,128)(2,1)S(1)} %dynamic_update_slice.27, bf16[2,1,256,256]{3,1,2,0:T(2,128)(2,1)S(1)} %copy.23, s32[]{:T(128)} %constant.72.clone.1, s32[]{:T(128)S(6)} %select_n.111, s32[]{:T(128)} %constant.72.clone.1, s32[]{:T(128)} %constant.72.clone.1) | dynamic-update-slice | bytes 524292 | tf_op jit(solution)/shard_map/dynamic_update_slice | solution.py:15
  99.9 7.1 %dynamic_update_slice.29 = bf16[2,8,256,256]{3,1,2,0:T(8,128)(2,1)S(1)} dynamic-update-slice(bf16[2,8,256,256]{3,1,2,0:T(8,128)(2,1)S(1)} %dynamic_update_slice.28, bf16[2,1,256,256]{3,1,2,0:T(2,128)(2,1)S(1)} %copy.24, s32[]{:T(128)} %constant.72.clone.1, s32[]{:T(128)S(6)} %select_n.113, s32[]{:T(128)} %constant.72.clone.1, s32[]{:T(128)} %constant.72.clone.1) | dynamic-update-slice | bytes 524292 | tf_op jit(solution)/shard_map/dynamic_update_slice | solution.py:15
  107.0 1.4 copy.25
  108.4 7.1 %dynamic_update_slice.30 = bf16[2,8,256,256]{3,1,2,0:T(8,128)(2,1)S(1)} dynamic-update-slice(bf16[2,8,256,256]{3,1,2,0:T(8,128)(2,1)S(1)} %dynamic_update_slice.29, bf16[2,1,256,256]{3,1,2,0:T(2,128)(2,1)S(1)} %copy.25, s32[]{:T(128)} %constant.72.clone.1, s32[]{:T(128)S(6)} %select_n.115, s32[]{:T(128)} %constant.72.clone.1, s32[]{:T(128)} %constant.72.clone.1) | dynamic-update-slice | bytes 524292 | tf_op jit(solution)/shard_map/dynamic_update_slice | solution.py:15
  115.6 1.4 copy.26
  116.9 7.1 %dynamic_update_slice.31 = bf16[2,8,256,256]{3,1,2,0:T(8,128)(2,1)S(1)} dynamic-update-slice(bf16[2,8,256,256]{3,1,2,0:T(8,128)(2,1)S(1)} %dynamic_update_slice.30, bf16[2,1,256,256]{3,1,2,0:T(2,128)(2,1)S(1)} %copy.26, s32[]{:T(128)} %constant.72.clone.1, s32[]{:T(128)S(6)} %select_n.117, s32[]{:T(128)} %constant.72.clone.1, s32[]{:T(128)} %constant.72.clone.1) | dynamic-update-slice | bytes 524292 | tf_op jit(solution)/shard_map/dynamic_update_slice | solution.py:15
  124.1 0.8 fusion.14
  124.8 0.8 copy-done.1
  125.7 1.9 %broadcast_select_fusion.1 = (bf16[2,8,256,256]{3,2,1,0:T(8,128)(2,1)S(1)}, bf16[2,8,256,256]{3,2,1,0:T(8,128)(2,1)S(1)}) fusion(bf16[2,8,256,256]{3,2,1,0:T(8,128)(2,1)S(1)} %copy-done.1, bf16[2,8,256,256]{3,2,1,0:T(8,128)(2,1)} %collective-permute-done, pred[]{:T(512)S(6)} %eq.28), kind=kLoop, calls=%fused_computation.9 | loop fusion | flops 2097152 | bytes 8388609 | tf_op jit(solution)/shard_map/jit(_where)/select_n | solution.py:42
  127.5 2.3 %pad_maximum_fusion = bf16[2,16,256,256]{3,2,1,0:T(8,128)(2,1)} fusion(bf16[2,8,256,256]{3,2,1,0:T(8,128)(2,1)S(1)} %get-tuple-element.3, bf16[2,8,256,256]{3,2,1,0:T(8,128)(2,1)S(1)} %get-tuple-element.2), kind=kLoop, calls=%fused_computation.2 | loop fusion | flops 2097152 | bytes 8388608 | tf_op jit(solution)/shard_map/concatenate | solution.py:44
  129.8 5.0 %gather_fusion.1 = bf16[16,2,256,256]{3,2,1,0:T(8,128)(2,1)} fusion(bf16[2,16,256,256]{3,2,1,0:T(8,128)(2,1)} %pad_maximum_fusion, s32[1024]{0:T(1024)S(1)} %pad_clamp_fusion), kind=kCustom, calls=%fused_computation.1 | custom fusion | bytes 8388672 | tf_op jit(solution)/shard_map/jit(_take)/gather | solution.py:45
  134.8 4.3 %fusion.13 = (f32[2,256]{1,0:T(2,128)S(1)}, bf16[2,2,256,256]{3,2,1,0:T(8,128)(2,1)}) fusion(f32[2,2,256,256]{3,1,2,0:T(2,128)S(1)} %fusion.14, bf16[2,8,256,256,1]{3,1,2,0,4:T(8,128)(2,1)S(1)} %bitcast.21, bf16[2,2,8,256,256]{4,3,0,2,1:T(8,128)(2,1)} %bitcast.22, pred[2,8]{1,0:T(4,128)(4,1)S(1)} %compare_and_fusion, pred[2,2]{1,0:T(4,128)(4,1)S(1)} %compare_reduce_fusion), kind=kOutput, calls=%fused_computation.14 | convolution fusion | flops 1077149184 | bytes 7866388 | tf_op jit(solution)/shard_map/iskxy,skyw->sixw/dot_general | solution.py:24
  139.1 21.7 %psum.7 = f32[2,256]{1,0:T(2,128)S(1)} all-reduce(f32[2,256]{1,0:T(2,128)S(1)} %get-tuple-element.4), channel_id=1, replica_groups=mesh['fields'=2,'prow'=8,'pcol'=2] {'prow'}, use_global_device_ids=true, to_apply=%region_2.3 | all-reduce | flops 512 | bytes 4096 | tf_op jit(solution)/shard_map/psum | solution.py:50
  160.8 0.6 sub.31
  (32 shorter events, 1.0 us)
Async XLA Ops:
  0.6 42.0 %copy-start = (s32[16]{0:T(128)S(1)}, s32[16]{0:T(128)}, u32[]{:S(2)}) copy-start(s32[16]{0:T(128)} %param.9) | copy-start | bytes 196
  0.6 12.6 %collective-permute-start.1 = (bf16[2,1,256,256]{3,2,1,0:T(8,128)(2,1)}, bf16[2,1,256,256]{3,2,1,0:T(8,128)(2,1)S(1)}, u32[]{:S(2)}, u32[]{:S(2)}) collective-permute-start(bf16[2,1,256,256]{3,2,1,0:T(8,128)(2,1)} %param.6), channel_id=1, source_target_pairs={{0,2},{2,4},{4,6},{6,8},{8,10},{10,12},{12,14},{14,0},{1,3},{3,5},... | collective-permute-start | bytes 786440 | tf_op jit(solution)/shard_map/ppermute | solution.py:14
  13.2 10.2 %collective-permute-start.2 = (bf16[2,1,256,256]{3,2,1,0:T(8,128)(2,1)S(1)}, bf16[2,1,256,256]{3,2,1,0:T(8,128)(2,1)S(1)}, u32[]{:S(2)}, u32[]{:S(2)}) collective-permute-start(bf16[2,1,256,256]{3,2,1,0:T(8,128)(2,1)S(1)} %collective-permute-done.1), channel_id=1, source_target_pairs={{0,2},{2,4},{4,6},{6,8},{8,10},{10,12},{12,14},{14,0},{1,3},{3,5},... | collective-permute-start | bytes 786440 | tf_op jit(solution)/shard_map/ppermute | solution.py:14
  13.3 111.6 %collective-permute-start = (bf16[2,8,256,256]{3,2,1,0:T(8,128)(2,1)}, bf16[2,8,256,256]{3,2,1,0:T(8,128)(2,1)}, u32[]{:S(2)}, u32[]{:S(2)}) collective-permute-start(bf16[2,8,256,256]{3,2,1,0:T(8,128)(2,1)} %param.5), channel_id=1, source_target_pairs={{0,1},{1,0},{2,3},{3,2},{4,5},{5,4},{6,7},{7,6},{8,9},{9,8},{10,11... | collective-permute-start | bytes 6291464 | tf_op jit(solution)/shard_map/ppermute | solution.py:20
  23.4 9.3 %collective-permute-start.3 = (bf16[2,1,256,256]{3,2,1,0:T(8,128)(2,1)S(1)}, bf16[2,1,256,256]{3,2,1,0:T(8,128)(2,1)S(1)}, u32[]{:S(2)}, u32[]{:S(2)}) collective-permute-start(bf16[2,1,256,256]{3,2,1,0:T(8,128)(2,1)S(1)} %collective-permute-done.2), channel_id=1, source_target_pairs={{0,2},{2,4},{4,6},{6,8},{8,10},{10,12},{12,14},{14,0},{1,3},{3,5},... | collective-permute-start | bytes 786440 | tf_op jit(solution)/shard_map/ppermute | solution.py:14
  32.7 9.1 %collective-permute-start.4 = (bf16[2,1,256,256]{3,2,1,0:T(8,128)(2,1)S(1)}, bf16[2,1,256,256]{3,2,1,0:T(8,128)(2,1)S(1)}, u32[]{:S(2)}, u32[]{:S(2)}) collective-permute-start(bf16[2,1,256,256]{3,2,1,0:T(8,128)(2,1)S(1)} %collective-permute-done.3), channel_id=1, source_target_pairs={{0,2},{2,4},{4,6},{6,8},{8,10},{10,12},{12,14},{14,0},{1,3},{3,5},... | collective-permute-start | bytes 786440 | tf_op jit(solution)/shard_map/ppermute | solution.py:14
  41.8 20.1 %copy-start.2 = (bf16[2,1,256,256]{3,2,1,0:T(8,128)(2,1)}, bf16[2,1,256,256]{3,2,1,0:T(8,128)(2,1)S(1)}, u32[]{:S(2)}) copy-start(bf16[2,1,256,256]{3,2,1,0:T(8,128)(2,1)S(1)} %collective-permute-done.4) | copy-start | bytes 786436
  41.8 9.1 %collective-permute-start.5 = (bf16[2,1,256,256]{3,2,1,0:T(8,128)(2,1)S(1)}, bf16[2,1,256,256]{3,2,1,0:T(8,128)(2,1)S(1)}, u32[]{:S(2)}, u32[]{:S(2)}) collective-permute-start(bf16[2,1,256,256]{3,2,1,0:T(8,128)(2,1)S(1)} %collective-permute-done.4), channel_id=1, source_target_pairs={{0,2},{2,4},{4,6},{6,8},{8,10},{10,12},{12,14},{14,0},{1,3},{3,5},... | collective-permute-start | bytes 786440 | tf_op jit(solution)/shard_map/ppermute | solution.py:14
  50.9 11.0 %copy-start.4 = (bf16[2,1,256,256]{3,2,1,0:T(8,128)(2,1)}, bf16[2,1,256,256]{3,2,1,0:T(8,128)(2,1)S(1)}, u32[]{:S(2)}) copy-start(bf16[2,1,256,256]{3,2,1,0:T(8,128)(2,1)S(1)} %collective-permute-done.5) | copy-start | bytes 786436
  50.9 9.5 %collective-permute-start.6 = (bf16[2,1,256,256]{3,2,1,0:T(8,128)(2,1)S(1)}, bf16[2,1,256,256]{3,2,1,0:T(8,128)(2,1)}, u32[]{:S(2)}, u32[]{:S(2)}) collective-permute-start(bf16[2,1,256,256]{3,2,1,0:T(8,128)(2,1)S(1)} %collective-permute-done.5), channel_id=1, source_target_pairs={{0,2},{2,4},{4,6},{6,8},{8,10},{10,12},{12,14},{14,0},{1,3},{3,5},... | collective-permute-start | bytes 786440 | tf_op jit(solution)/shard_map/ppermute | solution.py:14
  60.3 55.2 %collective-permute-start.7 = (bf16[2,1,256,256]{3,2,1,0:T(8,128)(2,1)}, bf16[2,1,256,256]{3,2,1,0:T(8,128)(2,1)}, u32[]{:S(2)}, u32[]{:S(2)}) collective-permute-start(bf16[2,1,256,256]{3,2,1,0:T(8,128)(2,1)} %collective-permute-done.6), channel_id=1, source_target_pairs={{0,2},{2,4},{4,6},{6,8},{8,10},{10,12},{12,14},{14,0},{1,3},{3,5},... | collective-permute-start | bytes 786440 | tf_op jit(solution)/shard_map/ppermute | solution.py:14
  76.8 15.1 %copy-start.3 = (bf16[2,1,256,256]{3,2,1,0:T(8,128)(2,1)S(1)}, bf16[2,1,256,256]{3,2,1,0:T(8,128)(2,1)}, u32[]{:S(2)}) copy-start(bf16[2,1,256,256]{3,2,1,0:T(8,128)(2,1)} %copy-done.2) | copy-start | bytes 786436
  84.3 15.1 %copy-start.5 = (bf16[2,1,256,256]{3,2,1,0:T(8,128)(2,1)S(1)}, bf16[2,1,256,256]{3,2,1,0:T(8,128)(2,1)}, u32[]{:S(2)}) copy-start(bf16[2,1,256,256]{3,2,1,0:T(8,128)(2,1)} %copy-done.4) | copy-start | bytes 786436
  124.1 1.6 copy-start.1
  134.8 26.0 %copy-start.6 = (f32[2,256]{1,0:T(2,128)S(1)}, f32[2,256]{1,0:T(2,128)}, u32[]{:S(2)}) copy-start(f32[2,256]{1,0:T(2,128)} %param.7) | copy-start | bytes 6148
